TPU v7x, 32 devices: a whole 2x2x4 slice. The times are simulated.
32 devices in a mesh: dp: 8 (over z, x), mp: 4 (over y, core).
Axes of the slice: x: 2, y: 2, z: 4, core: 2. Of those that a mesh axis runs over, the one named last changes fastest.
Arguments:
- media: bfloat16 [16, 8, 256, 1024], P('dp'), may hold values from -6 to 6
- latents: bfloat16 [64, 1024], replicated, may hold values from -6 to 6
- time_embed: bfloat16 [8, 1024], replicated, may hold values from -5 to 5
- media_gain: float32 [2, 1024], replicated, may hold values from 0.25 to 1.75
- latent_gain: float32 [2, 1024], replicated, may hold values from 0.25 to 1.75
- ffn_gain: float32 [2, 1024], replicated, may hold values from 0.25 to 1.75
- out_gain: float32 [1024], replicated, may hold values from 0.25 to 1.75
- w_query: bfloat16 [2, 1024, 512], P(None, 'dp', 'mp'), may hold values from -0.1875 to 0.1875
- w_key: bfloat16 [2, 1024, 512], P(None, 'dp', 'mp'), may hold values from -0.1875 to 0.1875
- w_value: bfloat16 [2, 1024, 512], P(None, 'dp', 'mp'), may hold values from -0.1875 to 0.1875
- w_out: bfloat16 [2, 512, 1024], P(None, 'mp', 'dp'), may hold values from -0.25 to 0.25
- w_up: bfloat16 [2, 1024, 4096], P(None, 'dp', 'mp'), may hold values from -0.1875 to 0.1875
- w_down: bfloat16 [2, 4096, 1024], P(None, 'mp', 'dp'), may hold values from -0.09375 to 0.09375
Outputs:
- resampled: bfloat16 [16, 64, 1024], P('dp')
All inputs are finite; a program needn't handle non-finite values.
Results may differ from a plain program's by a relative error of at most 0.013.
Values may be sent and summed in bfloat16 or wider, within the bound.
A program may use at most 128 MiB of HBM per device.

v0:
```python
import jax
import jax.numpy as jnp
from jax import lax
from jax.sharding import PartitionSpec as P

HEAD = 64
LAYERS = 2


def layer_norm(values, gain):
    center = values - jnp.mean(values, axis=-1, keepdims=True)
    spread = jnp.mean(center * center, axis=-1, keepdims=True)
    return center * lax.rsqrt(spread + 1e-05) * gain


def matmul(left, right):
    return jnp.dot(left, right, preferred_element_type=jnp.float32)


def on_device(
    media,
    latents,
    time_embed,
    media_gain,
    latent_gain,
    ffn_gain,
    out_gain,
    w_query,
    w_key,
    w_value,
    w_out,
    w_up,
    w_down,
):
    samples = media.shape[0]
    frames = media.shape[1]
    patches = media.shape[2]
    width = media.shape[3]
    count = latents.shape[0]
    head_size = HEAD
    local_heads = w_query.shape[2] // head_size
    scale = head_size ** (-0.5)
    tokens = frames * patches
    flat = (media.astype(jnp.float32) + time_embed.astype(jnp.float32)[None, :, None, :]).reshape(
        samples * tokens, width
    )
    state = jnp.broadcast_to(latents.astype(jnp.float32)[None], (samples, count, width)).reshape(
        samples * count, width
    )
    row_parts = (
        lax.all_gather(w_query, "dp", axis=1, tiled=True),
        lax.all_gather(w_key, "dp", axis=1, tiled=True),
        lax.all_gather(w_value, "dp", axis=1, tiled=True),
        lax.all_gather(w_up, "dp", axis=1, tiled=True),
    )
    col_parts = (
        lax.all_gather(w_out, "dp", axis=2, tiled=True),
        lax.all_gather(w_down, "dp", axis=2, tiled=True),
    )

    def full_rows(values, gain):
        normed = layer_norm(values, gain).astype(jnp.bfloat16)
        return normed

    def add_update(current, partial_value):
        return current + lax.psum(partial_value.astype(jnp.bfloat16), "mp").astype(jnp.float32)

    for layer in range(LAYERS):
        query_weight = row_parts[0][layer]
        key_weight = row_parts[1][layer]
        value_weight = row_parts[2][layer]
        up_weight = row_parts[3][layer]
        out_weight = col_parts[0][layer]
        down_weight = col_parts[1][layer]
        media_normed = layer_norm(flat, media_gain[layer]).astype(jnp.bfloat16)
        latent_normed = full_rows(state, latent_gain[layer])
        query = matmul(latent_normed, query_weight)
        key_media = matmul(media_normed, key_weight)
        value_media = matmul(media_normed, value_weight)
        key_latent = matmul(latent_normed, key_weight)
        value_latent = matmul(latent_normed, value_weight)
        queries = (
            (query * scale).astype(jnp.bfloat16).reshape(samples, count, local_heads, head_size)
        )
        keys = jnp.concatenate(
            [
                key_media.astype(jnp.bfloat16).reshape(samples, tokens, local_heads, head_size),
                key_latent.astype(jnp.bfloat16).reshape(samples, count, local_heads, head_size),
            ],
            axis=1,
        )
        values = jnp.concatenate(
            [
                value_media.astype(jnp.bfloat16).reshape(samples, tokens, local_heads, head_size),
                value_latent.astype(jnp.bfloat16).reshape(samples, count, local_heads, head_size),
            ],
            axis=1,
        )
        scores = jnp.einsum("sqhd,skhd->shqk", queries, keys, preferred_element_type=jnp.float32)
        probs = jax.nn.softmax(scores, axis=-1).astype(jnp.bfloat16)
        attended = jnp.einsum("shqk,skhd->sqhd", probs, values, preferred_element_type=jnp.float32)
        attended = attended.astype(jnp.bfloat16).reshape(samples * count, local_heads * head_size)
        state = add_update(state, matmul(attended, out_weight))
        ffn_normed = full_rows(state, ffn_gain[layer])
        hidden = jax.nn.gelu(matmul(ffn_normed, up_weight), approximate=False).astype(jnp.bfloat16)
        state = add_update(state, matmul(hidden, down_weight))
    final = layer_norm(state, out_gain).astype(jnp.bfloat16)
    return final.reshape(samples, count, width)


def solution(mesh):
    in_specs = (
        P("dp", None, None, None),
        P(),
        P(),
        P(),
        P(),
        P(),
        P(),
        P(None, "dp", "mp"),
        P(None, "dp", "mp"),
        P(None, "dp", "mp"),
        P(None, "mp", "dp"),
        P(None, "dp", "mp"),
        P(None, "mp", "dp"),
    )
    out_specs = P("dp", None, None)
    return jax.shard_map(
        on_device, mesh=mesh, in_specs=in_specs, out_specs=out_specs, check_vma=False
    )
```

profile of v0, /device:TPU:0, one launch (start us, length us, event | category | flops | bytes accessed | tf_op | source)
XLA Modules:
  0.0 459.3 jit_solution(7624220394603291275)
XLA Ops:
  10.3 33.3 %all_gather.20 = bf16[2,1024,128]{2,1,0:T(8,128)(2,1)S(1)} all-gather(bf16[2,128,128]{2,1,0:T(8,128)(2,1)} %param.21), channel_id=1, replica_groups=mesh['dp'=8,'mp'=4] {'dp'}, dimensions={1}, use_global_device_ids=true | all-gather | bytes 589824 | tf_op jit(solution)/shard_map/all_gather | solution.py:52
  44.3 5.3 %fusion.3 = f32[2,8,256]{2,1,0:T(8,128)S(1)} fusion(bf16[2,8,256,1024]{3,2,1,0:T(8,128)(2,1)} %param.13, f32[8,1024]{1,0:T(8,128)S(1)} %convert_element_type.135), kind=kLoop, calls=%fused_computation.7 | loop fusion | flops 12578816 | bytes 8437760 | tf_op jit(solution)/shard_map/reduce_sum | solution.py:11
  53.7 5.8 %multiply_convert_fusion = (bf16[2,8,256,1024]{3,2,1,0:T(8,128)(2,1)}, bf16[2,8,256,1024]{3,2,1,0:T(8,128)(2,1)S(1)}) fusion(bf16[2,8,256,1024]{3,2,1,0:T(8,128)(2,1)S(1)} %copy-done, f32[1024]{0:T(1024)S(1)} %bitcast.110, f32[2,8,256]{2,1,0:T(8,128)S(1)} %add_rsqrt_fusion, f32[2,8,256]{2,1,0:T(8,128)S(1)} %broadcast_multiply_fusion, ...), kind=kLoop, calls=%fused_computation.2 | loop fusion | flops 33554432 | bytes 25239552 | tf_op jit(solution)/shard_map/convert_element_type | solution.py:75
  62.9 31.3 %all_gather.18 = bf16[2,1024,128]{2,1,0:T(8,128)(2,1)S(1)} all-gather(bf16[2,128,128]{2,1,0:T(8,128)(2,1)S(1)} %copy-done.12), channel_id=1, replica_groups=mesh['dp'=8,'mp'=4] {'dp'}, dimensions={1}, use_global_device_ids=true | all-gather | bytes 589824 | tf_op jit(solution)/shard_map/all_gather | solution.py:53
  98.6 31.6 %all_gather.19 = bf16[2,1024,128]{2,1,0:T(8,128)(2,1)S(1)} all-gather(bf16[2,128,128]{2,1,0:T(8,128)(2,1)S(1)} %copy-done.13), channel_id=1, replica_groups=mesh['dp'=8,'mp'=4] {'dp'}, dimensions={1}, use_global_device_ids=true | all-gather | bytes 589824 | tf_op jit(solution)/shard_map/all_gather | solution.py:51
  131.1 3.9 reshape.424
  135.0 3.5 copy.28
  138.7 3.9 reshape.423
  142.6 3.5 copy.25
  151.9 27.0 %all_gather.21 = bf16[2,128,1024]{2,1,0:T(8,128)(2,1)S(1)} all-gather(bf16[2,128,128]{2,1,0:T(8,128)(2,1)S(1)} %copy-done.14), channel_id=1, replica_groups=mesh['dp'=8,'mp'=4] {'dp'}, dimensions={2}, use_global_device_ids=true | all-gather | bytes 589824 | tf_op jit(solution)/shard_map/all_gather | solution.py:57
  182.0 6.8 %convolution_convert_fusion = bf16[4096,128]{1,0:T(8,128)(2,1)} fusion(bf16[4096,1024]{1,0:T(8,128)(2,1)} %bitcast.100, bf16[2,1024,128]{2,1,0:T(8,128)(2,1)S(1)} %all_gather.20), kind=kOutput, calls=%fused_computation.9 | convolution fusion | flops 1074266112 | bytes 9699328 | tf_op jit(solution)/shard_map/dot_general | solution.py:17
  188.7 23.7 %all-reduce.5.cloned.1.call-done = bf16[128,1024]{1,0:T(8,128)(2,1)} async-done(((bf16[128,1024]{1,0:T(8,128)(2,1)}), bf16[128,1024]{1,0:T(8,128)(2,1)}) %all-reduce.5.cloned.1.call-update) | async-done | bytes 262160 | tf_op jit(solution)/shard_map/psum | solution.py:66
  215.9 39.4 %all-gather.3.cloned.1.call-done = bf16[2,1024,1024]{2,1,0:T(8,128)(2,1)} async-done(((bf16[2,128,1024]{2,1,0:T(8,128)(2,1)}), bf16[2,1024,1024]{2,1,0:T(8,128)(2,1)}) %all-gather.3.cloned.1.call-update) | async-done | bytes 4194320 | tf_op jit(solution)/shard_map/all_gather | solution.py:54
  255.3 75.0 %all-gather.5.cloned.1.call-done = bf16[2,1024,1024]{2,1,0:T(8,128)(2,1)} async-done(((bf16[2,1024,128]{2,1,0:T(8,128)(2,1)}), bf16[2,1024,1024]{2,1,0:T(8,128)(2,1)}) %all-gather.5.cloned.1.call-update) | async-done | bytes 4194320 | tf_op jit(solution)/shard_map/all_gather | solution.py:58
  330.3 4.8 %fusion.13 = bf16[128,1024]{1,0:T(8,128)(2,1)} fusion(bf16[2,1024,1024]{2,1,0:T(8,128)(2,1)} %all-gather.5.cloned.1.call-done, bf16[128,1024]{1,0:T(8,128)(2,1)S(1)} %multiply_convert_fusion.5, bf16[2,1024,1024]{2,1,0:T(8,128)(2,1)} %all-gather.3.cloned.1.call-done), kind=kOutput, calls=%fused_computation.27 | convolution fusion | flops 545521664 | bytes 4718592 | tf_op jit(solution)/shard_map/dot_general | solution.py:17
  335.4 6.7 %convolution_convert_fusion.1 = bf16[4096,128]{1,0:T(8,128)(2,1)} fusion(bf16[4096,1024]{1,0:T(8,128)(2,1)} %bitcast.101, bf16[2,1024,128]{2,1,0:T(8,128)(2,1)S(1)} %copy-done.4), kind=kOutput, calls=%fused_computation.10 | convolution fusion | flops 1074266112 | bytes 9699328 | tf_op jit(solution)/shard_map/dot_general | solution.py:17
  342.1 3.9 reshape.426
  346.0 3.5 copy.36
  349.5 3.9 reshape.425
  353.4 3.6 copy.33
  357.0 8.7 %all-reduce.7.cloned.1.call-done = bf16[128,1024]{1,0:T(8,128)(2,1)} async-done(((bf16[128,1024]{1,0:T(8,128)(2,1)}), bf16[128,1024]{1,0:T(8,128)(2,1)}) %all-reduce.7.cloned.1.call-update) | async-done | bytes 262160 | tf_op jit(solution)/shard_map/psum | solution.py:66
  377.0 32.4 %all-reduce.9.cloned.1.call-done = bf16[128,1024]{1,0:T(8,128)(2,1)} async-done(((bf16[128,1024]{1,0:T(8,128)(2,1)}), bf16[128,1024]{1,0:T(8,128)(2,1)}) %all-reduce.9.cloned.1.call-update) | async-done | bytes 262160 | tf_op jit(solution)/shard_map/psum | solution.py:66
  410.8 4.9 %fusion.14 = bf16[128,1024]{1,0:T(8,128)(2,1)} fusion(bf16[2,1024,1024]{2,1,0:T(8,128)(2,1)} %all-gather.5.cloned.1.call-done, bf16[2,1024,1024]{2,1,0:T(8,128)(2,1)} %all-gather.3.cloned.1.call-done, f32[128,1024]{1,0:T(8,128)S(1)} %get-tuple-element.6, f32[1024]{0:T(1024)S(1)} %bitcast.112, f32[128]{0:T(128)S(1)} %add_rsqrt_fusion.3, ...), kind=kOutput, calls=%fused_computation.28 | convolution fusion | flops 546045952 | bytes 4985856 | tf_op jit(solution)/shard_map/dot_general | solution.py:17
  415.7 32.4 %all-reduce.11.cloned.1.call-done = bf16[128,1024]{1,0:T(8,128)(2,1)} async-done(((bf16[128,1024]{1,0:T(8,128)(2,1)}), bf16[128,1024]{1,0:T(8,128)(2,1)}) %all-reduce.11.cloned.1.call-update) | async-done | bytes 262160 | tf_op jit(solution)/shard_map/psum | solution.py:66
  (108 shorter events, 45.7 us)
Async XLA Ops:
  7.4 205.1 %all-reduce.5.cloned.1.call-start = ((), (), s32[]{:S(2)}) async-start(), calls=%async_computation | async-start | bytes 524288 | tf_op jit(solution)/shard_map/psum | solution.py:66
  44.3 5.8 %copy-start = (bf16[2,8,256,1024]{3,2,1,0:T(8,128)(2,1)S(1)}, bf16[2,8,256,1024]{3,2,1,0:T(8,128)(2,1)}, u32[]{:S(2)}) copy-start(bf16[2,8,256,1024]{3,2,1,0:T(8,128)(2,1)} %param.13) | copy-start | bytes 25165828
  50.1 3.2 copy-start.15
  59.4 3.4 copy-start.12
  94.1 0.8 copy-start.3
  94.9 3.7 copy-start.13
  130.2 0.8 copy-start.10
  146.1 3.4 copy-start.9
  149.5 2.4 copy-start.14
  151.7 30.2 %copy-start.16 = (f32[2,1024]{1,0:T(2,128)S(1)}, f32[2,1024]{1,0:T(2,128)}, u32[]{:S(2)}) copy-start(f32[2,1024]{1,0:T(2,128)} %param.18) | copy-start | bytes 24580
  179.0 0.8 copy-start.6
  180.7 74.5 %all-gather.3.cloned.1.call-start = ((), (), s32[]{:S(2)}) async-start(), calls=%async_computation.1 | async-start | bytes 4718592 | tf_op jit(solution)/shard_map/all_gather | solution.py:54
  181.3 149.0 %all-gather.5.cloned.1.call-start = ((), (), s32[]{:S(2)}) async-start(), calls=%async_computation.2 | async-start | bytes 4718592 | tf_op jit(solution)/shard_map/all_gather | solution.py:58
  181.9 183.8 %all-reduce.7.cloned.1.call-start = ((), (), s32[]{:S(2)}) async-start(), calls=%async_computation.3 | async-start | bytes 524288 | tf_op jit(solution)/shard_map/psum | solution.py:66
  215.9 119.5 %copy-start.4 = (bf16[2,1024,128]{2,1,0:T(8,128)(2,1)S(1)}, bf16[2,1024,128]{2,1,0:T(8,128)(2,1)}, u32[]{:S(2)}) copy-start(bf16[2,1024,128]{2,1,0:T(8,128)(2,1)} %copy-done.3) | copy-start | bytes 1572868
  335.1 74.3 %all-reduce.9.cloned.1.call-start = ((), (), s32[]{:S(2)}) async-start(), calls=%async_computation.4 | async-start | bytes 524288 | tf_op jit(solution)/shard_map/psum | solution.py:66
  353.4 12.3 %copy-start.1 = (bf16[128,1024]{1,0:T(8,128)(2,1)S(1)}, bf16[128,1024]{1,0:T(8,128)(2,1)}, u32[]{:S(2)}) copy-start(bf16[128,1024]{1,0:T(8,128)(2,1)} %all-reduce.5.cloned.1.call-done) | copy-start | bytes 786436
  357.0 12.4 %copy-start.11 = (bf16[2,1024,128]{2,1,0:T(8,128)(2,1)S(1)}, bf16[2,1024,128]{2,1,0:T(8,128)(2,1)}, u32[]{:S(2)}) copy-start(bf16[2,1024,128]{2,1,0:T(8,128)(2,1)} %copy-done.10) | copy-start | bytes 1572868
  357.0 12.6 %copy-start.5 = (bf16[2,1024,128]{2,1,0:T(8,128)(2,1)S(1)}, bf16[2,1024,128]{2,1,0:T(8,128)(2,1)}, u32[]{:S(2)}) copy-start(bf16[2,1024,128]{2,1,0:T(8,128)(2,1)} %copy-done.3) | copy-start | bytes 1572868
  369.8 3.8 copy-start.8
  373.6 2.5 copy-start.7
  373.6 35.9 %copy-start.2 = (bf16[128,1024]{1,0:T(8,128)(2,1)S(1)}, bf16[128,1024]{1,0:T(8,128)(2,1)}, u32[]{:S(2)}) copy-start(bf16[128,1024]{1,0:T(8,128)(2,1)} %all-reduce.7.cloned.1.call-done) | copy-start | bytes 786436
  377.0 71.1 %all-reduce.11.cloned.1.call-start = ((), (), s32[]{:S(2)}) async-start(), calls=%async_computation.5 | async-start | bytes 524288 | tf_op jit(solution)/shard_map/psum | solution.py:66
  410.8 39.6 %copy-start.17 = (f32[1024]{0:T(1024)S(1)}, f32[1024]{0:T(1024)}, u32[]{:S(2)}) copy-start(f32[1024]{0:T(1024)} %param.19) | copy-start | bytes 12292
Sparse Core Ops, SparseCore 0:
  180.8 31.5 all-reduce.4
  335.2 30.4 all-reduce.6
  377.1 32.2 all-reduce.8
  415.8 32.2 all-reduce.10
Sparse Core Ops, SparseCore 1:
  183.4 71.8 all-gather.2
  257.2 73.0 all-gather.4
where the time goes:
time: 460 us; the launch traced here: 459 us
  waiting for transfers between devices  213 us (46%)
  blocking collectives  123 us (27%)
  matrix products  44.2 us (10%)
  local copies, waits for them, and re-layouts  34.3 us (7%)
  other arithmetic  29.4 us (6%)
  between operations  15 us (3%)
    psum x4, waiting for transfers between devices, add_update(): lax.psum(partial_value.astype(jnp.bfloat16), 'mp').astype(jnp.float32)  97.3 us
    all_gather x1, waiting for transfers between devices, on_device(): lax.all_gather(w_down, 'dp', axis=2, tiled=True)  75 us
    all_gather x1, waiting for transfers between devices, on_device(): lax.all_gather(w_up, 'dp', axis=1, tiled=True)  39.4 us
    all_gather x1, blocking collectives, on_device(): lax.all_gather(w_key, 'dp', axis=1, tiled=True)  33.3 us
    dot_general x14, matrix products, matmul(): return jnp.dot(left, right, preferred_element_type=jnp.float32)  33.2 us
    all_gather x1, blocking collectives, on_device(): lax.all_gather(w_query, 'dp', axis=1, tiled=True)  31.6 us
    all_gather x1, blocking collectives, on_device(): lax.all_gather(w_value, 'dp', axis=1, tiled=True)  31.3 us
    all_gather x1, blocking collectives, on_device(): lax.all_gather(w_out, 'dp', axis=2, tiled=True)  27 us
  transfers between devices with their start and end apart: 6, of which 6 were waited for; matrix products, arithmetic and copies ran while one was open for 7% of the time, Pallas kernels for 0%

commit v1 on v0

--- a/solution.py
+++ b/solution.py
@@ -2,6 +2,7 @@
 import jax.numpy as jnp
 from jax import lax
 from jax.sharding import PartitionSpec as P
+from jax.lax import all_gather
 
 HEAD = 64
 LAYERS = 2
@@ -63,7 +64,9 @@
         return normed
 
     def add_update(current, partial_value):
-        return current + lax.psum(partial_value.astype(jnp.bfloat16), "mp").astype(jnp.float32)
+        return current + jnp.sum(all_gather(partial_value.astype(jnp.bfloat16), "mp"), 0).astype(
+            jnp.float32
+        )
 
     for layer in range(LAYERS):
         query_weight = row_parts[0][layer]

time: 460 us -> 436 us (0.948)
  waiting for transfers between devices: 213 us -> 196 us
    psum x4 -> x0, waiting for transfers between devices: 97.3 us -> none  [add_update(): lax.psum(partial_value.astype(jnp.bfloat16), 'mp').astype(jnp.float32)]
    all_gather x0 -> x4, waiting for transfers between devices: none -> 46.5 us  [add_update(): all_gather(partial_value.astype(jnp.bfloat16), 'mp')]
    all_gather x1, waiting for transfers between devices: 39.4 us -> 72.9 us  [on_device(): lax.all_gather(w_up, 'dp', axis=1, tiled=True)]
    reduce_sum x0 -> x4, other arithmetic: none -> 5.77 us  [add_update(): jnp.sum(all_gather(partial_value.astype(jnp.bfloat16), 'mp'), 0)]
  transfers between devices with their start and end apart: 6 -> 6, of which waited for: 6 -> 5; matrix products, arithmetic and copies ran while one was open for 7% -> 7% of each run, Pallas kernels for 0% -> 0%
where the time goes in v1:
time: 436 us
  waiting for transfers between devices  196 us (45%)
  blocking collectives  123 us (28%)
  matrix products  42.8 us (10%)
  local copies, waits for them, and re-layouts  33.3 us (8%)
  other arithmetic  25.8 us (6%)
  between operations  13.9 us (3%)
    all_gather x1, waiting for transfers between devices, on_device(): lax.all_gather(w_down, 'dp', axis=2, tiled=True)  75.3 us
    all_gather x1, waiting for transfers between devices, on_device(): lax.all_gather(w_up, 'dp', axis=1, tiled=True)  72.9 us
    all_gather x4, waiting for transfers between devices, add_update(): all_gather(partial_value.astype(jnp.bfloat16), 'mp')  46.5 us
    all_gather x1, blocking collectives, on_device(): lax.all_gather(w_key, 'dp', axis=1, tiled=True)  33.3 us
    dot_general x14, matrix products, matmul(): return jnp.dot(left, right, preferred_element_type=jnp.float32)  32.2 us
    all_gather x1, blocking collectives, on_device(): lax.all_gather(w_query, 'dp', axis=1, tiled=True)  31.4 us
    all_gather x1, blocking collectives, on_device(): lax.all_gather(w_value, 'dp', axis=1, tiled=True)  31.3 us
    all_gather x1, blocking collectives, on_device(): lax.all_gather(w_out, 'dp', axis=2, tiled=True)  27 us
  transfers between devices with their start and end apart: 6, of which 5 were waited for; matrix products, arithmetic and copies ran while one was open for 7% of the time, Pallas kernels for 0%

profile of v1, /device:TPU:0, one launch (start us, length us, event | category | flops | bytes accessed | tf_op | source)
XLA Modules:
  0.0 435.6 jit_solution(13901535496220445724)
XLA Ops:
  9.5 33.3 %all_gather.44 = bf16[2,1024,128]{2,1,0:T(8,128)(2,1)S(1)} all-gather(bf16[2,128,128]{2,1,0:T(8,128)(2,1)} %param.21), channel_id=1, replica_groups=mesh['dp'=8,'mp'=4] {'dp'}, dimensions={1}, use_global_device_ids=true | all-gather | bytes 589824 | tf_op jit(solution)/shard_map/all_gather | solution.py:53
  43.5 5.3 %fusion.3 = f32[2,8,256]{2,1,0:T(8,128)S(1)} fusion(bf16[2,8,256,1024]{3,2,1,0:T(8,128)(2,1)} %param.13, f32[8,1024]{1,0:T(8,128)S(1)} %convert_element_type.341), kind=kLoop, calls=%fused_computation.7 | loop fusion | flops 12578816 | bytes 8437760 | tf_op jit(solution)/shard_map/reduce_sum | solution.py:12
  52.9 5.8 %multiply_convert_fusion = (bf16[2,8,256,1024]{3,2,1,0:T(8,128)(2,1)}, bf16[2,8,256,1024]{3,2,1,0:T(8,128)(2,1)S(1)}) fusion(bf16[2,8,256,1024]{3,2,1,0:T(8,128)(2,1)S(1)} %copy-done, f32[1024]{0:T(1024)S(1)} %bitcast.133, f32[2,8,256]{2,1,0:T(8,128)S(1)} %add_rsqrt_fusion, f32[2,8,256]{2,1,0:T(8,128)S(1)} %broadcast_multiply_fusion, ...), kind=kLoop, calls=%fused_computation.2 | loop fusion | flops 33554432 | bytes 25239552 | tf_op jit(solution)/shard_map/convert_element_type | solution.py:78
  58.6 3.5 convolution_convert_fusion.2
  62.1 31.3 %all_gather.42 = bf16[2,1024,128]{2,1,0:T(8,128)(2,1)S(1)} all-gather(bf16[2,128,128]{2,1,0:T(8,128)(2,1)S(1)} %copy-done.13), channel_id=1, replica_groups=mesh['dp'=8,'mp'=4] {'dp'}, dimensions={1}, use_global_device_ids=true | all-gather | bytes 589824 | tf_op jit(solution)/shard_map/all_gather | solution.py:54
  97.5 31.4 %all_gather.43 = bf16[2,1024,128]{2,1,0:T(8,128)(2,1)S(1)} all-gather(bf16[2,128,128]{2,1,0:T(8,128)(2,1)S(1)} %copy-done.14), channel_id=1, replica_groups=mesh['dp'=8,'mp'=4] {'dp'}, dimensions={1}, use_global_device_ids=true | all-gather | bytes 589824 | tf_op jit(solution)/shard_map/all_gather | solution.py:52
  129.8 3.9 reshape.1028
  133.7 3.6 copy.28
  138.9 3.5 copy.25
  147.8 27.0 %all_gather.45 = bf16[2,128,1024]{2,1,0:T(8,128)(2,1)S(1)} all-gather(bf16[2,128,128]{2,1,0:T(8,128)(2,1)S(1)} %copy-done.15), channel_id=1, replica_groups=mesh['dp'=8,'mp'=4] {'dp'}, dimensions={2}, use_global_device_ids=true | all-gather | bytes 589824 | tf_op jit(solution)/shard_map/all_gather | solution.py:58
  178.2 14.9 %all-gather.15.cloned.1.call-done = bf16[512,1024]{1,0:T(8,128)(2,1)} async-done(((bf16[128,1024]{1,0:T(8,128)(2,1)}), bf16[512,1024]{1,0:T(8,128)(2,1)}) %all-gather.15.cloned.1.call-update) | async-done | bytes 1048592 | tf_op jit(solution)/shard_map/all_gather | solution.py:67
  195.3 72.9 %all-gather.11.cloned.1.call-done = bf16[2,1024,1024]{2,1,0:T(8,128)(2,1)} async-done(((bf16[2,128,1024]{2,1,0:T(8,128)(2,1)}), bf16[2,1024,1024]{2,1,0:T(8,128)(2,1)}) %all-gather.11.cloned.1.call-update) | async-done | bytes 4194320 | tf_op jit(solution)/shard_map/all_gather | solution.py:55
  268.1 75.3 %all-gather.13.cloned.1.call-done = bf16[2,1024,1024]{2,1,0:T(8,128)(2,1)} async-done(((bf16[2,1024,128]{2,1,0:T(8,128)(2,1)}), bf16[2,1024,1024]{2,1,0:T(8,128)(2,1)}) %all-gather.13.cloned.1.call-update) | async-done | bytes 4194320 | tf_op jit(solution)/shard_map/all_gather | solution.py:59
  343.4 4.8 %fusion.13 = bf16[128,1024]{1,0:T(8,128)(2,1)} fusion(bf16[2,1024,1024]{2,1,0:T(8,128)(2,1)} %all-gather.13.cloned.1.call-done, bf16[128,1024]{1,0:T(8,128)(2,1)S(1)} %bitcast.127, bf16[2,1024,1024]{2,1,0:T(8,128)(2,1)} %all-gather.11.cloned.1.call-done), kind=kOutput, calls=%fused_computation.27 | convolution fusion | flops 545521664 | bytes 4718592 | tf_op jit(solution)/shard_map/dot_general | solution.py:18
  348.5 6.7 %convolution_convert_fusion = bf16[4096,128]{1,0:T(8,128)(2,1)} fusion(bf16[4096,1024]{1,0:T(8,128)(2,1)} %bitcast.110, bf16[2,1024,128]{2,1,0:T(8,128)(2,1)S(1)} %copy-done.2), kind=kOutput, calls=%fused_computation.9 | convolution fusion | flops 1074266112 | bytes 9699328 | tf_op jit(solution)/shard_map/dot_general | solution.py:18
  355.3 3.9 reshape.1030
  359.2 3.6 copy.36
  362.7 6.7 %convolution_convert_fusion.1 = bf16[4096,128]{1,0:T(8,128)(2,1)} fusion(bf16[4096,1024]{1,0:T(8,128)(2,1)} %bitcast.111, bf16[2,1024,128]{2,1,0:T(8,128)(2,1)} %copy-done.4), kind=kOutput, calls=%fused_computation.10 | convolution fusion | flops 1074266112 | bytes 9699328 | tf_op jit(solution)/shard_map/dot_general | solution.py:18
  369.4 3.9 reshape.1029
  373.3 3.5 copy.33
  380.3 3.2 fusion.219
  387.3 14.8 %all-gather.19.cloned.1.call-done = bf16[512,1024]{1,0:T(8,128)(2,1)} async-done(((bf16[128,1024]{1,0:T(8,128)(2,1)}), bf16[512,1024]{1,0:T(8,128)(2,1)}) %all-gather.19.cloned.1.call-update) | async-done | bytes 1048592 | tf_op jit(solution)/shard_map/all_gather | solution.py:67
  404.3 4.8 %fusion.14 = bf16[128,1024]{1,0:T(8,128)(2,1)} fusion(bf16[2,1024,1024]{2,1,0:T(8,128)(2,1)} %all-gather.13.cloned.1.call-done, bf16[128,1024]{1,0:T(8,128)(2,1)S(1)} %bitcast.128, bf16[2,1024,1024]{2,1,0:T(8,128)(2,1)} %all-gather.11.cloned.1.call-done), kind=kOutput, calls=%fused_computation.28 | convolution fusion | flops 545521664 | bytes 4718592 | tf_op jit(solution)/shard_map/dot_general | solution.py:18
  409.1 16.8 %all-gather.21.cloned.1.call-done = bf16[512,1024]{1,0:T(8,128)(2,1)} async-done(((bf16[128,1024]{1,0:T(8,128)(2,1)}), bf16[512,1024]{1,0:T(8,128)(2,1)}) %all-gather.21.cloned.1.call-update) | async-done | bytes 1048592 | tf_op jit(solution)/shard_map/all_gather | solution.py:67
  (125 shorter events, 37.4 us)
Async XLA Ops:
  6.5 186.6 %all-gather.15.cloned.1.call-start = ((), (), s32[]{:S(2)}) async-start(), calls=%async_computation.2 | async-start | bytes 1310720 | tf_op jit(solution)/shard_map/all_gather | solution.py:67
  42.7 15.9 %copy-start.1 = (bf16[2,1024,128]{2,1,0:T(8,128)(2,1)}, bf16[2,1024,128]{2,1,0:T(8,128)(2,1)S(1)}, u32[]{:S(2)}) copy-start(bf16[2,1024,128]{2,1,0:T(8,128)(2,1)S(1)} %all_gather.44) | copy-start | bytes 1572868
  43.5 5.8 %copy-start = (bf16[2,8,256,1024]{3,2,1,0:T(8,128)(2,1)S(1)}, bf16[2,8,256,1024]{3,2,1,0:T(8,128)(2,1)}, u32[]{:S(2)}) copy-start(bf16[2,8,256,1024]{3,2,1,0:T(8,128)(2,1)} %param.13) | copy-start | bytes 25165828
  49.2 3.2 copy-start.17
  58.6 3.5 copy-start.13
  94.2 3.2 copy-start.14
  138.9 3.5 copy-start.9
  142.4 3.0 copy-start.10
  142.4 3.0 copy-start.16
  145.4 2.4 copy-start.15
  147.6 30.6 %copy-start.18 = (f32[2,1024]{1,0:T(2,128)S(1)}, f32[2,1024]{1,0:T(2,128)}, u32[]{:S(2)}) copy-start(f32[2,1024]{1,0:T(2,128)} %param.18) | copy-start | bytes 24580
  174.9 0.8 copy-start.6
  176.7 91.5 %all-gather.11.cloned.1.call-start = ((), (), s32[]{:S(2)}) async-start(), calls=%async_computation | async-start | bytes 4718592 | tf_op jit(solution)/shard_map/all_gather | solution.py:55
  177.4 166.0 %all-gather.13.cloned.1.call-start = ((), (), s32[]{:S(2)}) async-start(), calls=%async_computation.1 | async-start | bytes 4718592 | tf_op jit(solution)/shard_map/all_gather | solution.py:59
  178.1 198.7 %all-gather.17.cloned.1.call-start = ((), (), s32[]{:S(2)}) async-start(), calls=%async_computation.3 | async-start | bytes 1310720 | tf_op jit(solution)/shard_map/all_gather | solution.py:67
  343.4 5.1 %copy-start.2 = (bf16[2,1024,128]{2,1,0:T(8,128)(2,1)S(1)}, bf16[2,1024,128]{2,1,0:T(8,128)(2,1)}, u32[]{:S(2)}) copy-start(bf16[2,1024,128]{2,1,0:T(8,128)(2,1)} %copy-done.1) | copy-start | bytes 1572868
  348.3 53.8 %all-gather.19.cloned.1.call-start = ((), (), s32[]{:S(2)}) async-start(), calls=%async_computation.4 | async-start | bytes 1310720 | tf_op jit(solution)/shard_map/all_gather | solution.py:67
  376.8 2.2 copy-start.3
  378.3 1.0 copy-start.12
  378.3 1.3 copy-start.5
  379.8 3.8 copy-start.8
  383.6 2.4 copy-start.7
  387.0 39.0 %all-gather.21.cloned.1.call-start = ((), (), s32[]{:S(2)}) async-start(), calls=%async_computation.5 | async-start | bytes 1310720 | tf_op jit(solution)/shard_map/all_gather | solution.py:67
  409.1 18.8 %copy-start.19 = (f32[1024]{0:T(1024)S(1)}, f32[1024]{0:T(1024)}, u32[]{:S(2)}) copy-start(f32[1024]{0:T(1024)} %param.19) | copy-start | bytes 12292
  (2 other events, 1.6 us)
Sparse Core Ops, SparseCore 0:
  176.8 16.3 all-gather.14
  195.3 72.7 all-gather.10
  270.2 73.1 all-gather.12
  348.4 14.8 all-gather.16
  387.1 14.9 all-gather.18
  409.2 16.6 all-gather.20
